TPU v7x, 512 devices: a whole 4x8x8 slice. The times are simulated.
512 devices in a mesh: ep: 8 (over y), etp: 64 (over z, x, core).
Axes of the slice: x: 4, y: 8, z: 8, core: 2. Of those that a mesh axis runs over, the one named last changes fastest.
Arguments:
- tokens: bfloat16 [384, 3072], P('ep', 'etp'), may hold values from -6 to 6
- routes: int32 [384, 2], P('ep'), may hold values from 0 to 7, as said below
- route_gates: float32 [384, 2], P('ep'), may hold values from 0.1 to 0.9
- cotangent: bfloat16 [384, 3072], P('ep', 'etp'), may hold values from -1.5 to 1.5
- w_gate: bfloat16 [8, 3072, 8192], P('ep', None, 'etp'), may hold values from -0.109375 to 0.109375
- w_up: bfloat16 [8, 3072, 8192], P('ep', None, 'etp'), may hold values from -0.109375 to 0.109375
- w_down: bfloat16 [8, 8192, 3072], P('ep', 'etp'), may hold values from -0.1875 to 0.1875
Outputs:
- mixed: bfloat16 [384, 3072], P('ep', 'etp')
- grad_gates: float32 [384, 2], P('ep')
- grad_w_gate: bfloat16 [8, 3072, 8192], P('ep', None, 'etp')
- grad_w_up: bfloat16 [8, 3072, 8192], P('ep', None, 'etp')
- grad_w_down: bfloat16 [8, 8192, 3072], P('ep', 'etp')
Inputs may be any that keep to these rules, and one draw needn't show every extreme that they name: `routes`: within each aligned block of 48 rows (the tokens of one index of ep) the two experts of a row differ and no expert is named by more than 24 rows; one expert, the same in every block, is named by exactly 24 rows of each block.
All inputs are finite; a program needn't handle non-finite values.
Results may differ from a plain program's by a relative error of at most 0.0058.
Values may be sent and summed in bfloat16 or wider, within the bound.
A program may use at most 64 MiB of HBM per device.

v0:
```python
import jax
import jax.numpy as jnp
from jax import lax
from jax.sharding import PartitionSpec as P

EXPERTS = 8
CAP = 24


def per_device(tokens, routes, route_gates, cotangent, w_gate, w_up, w_down):
    local_experts = w_gate.shape[0]
    ep_count = lax.axis_size("ep")
    tok_count = tokens.shape[0]
    flat_ids = routes.reshape(-1)
    pair_count = flat_ids.shape[0]
    onehot = (flat_ids[:, None] == jnp.arange(EXPERTS, dtype=jnp.int32)[None, :]).astype(jnp.int32)
    before = jnp.cumsum(onehot, axis=0) - onehot
    slot_id = jnp.sum(before * onehot, axis=1)
    target = flat_ids * CAP + slot_id
    slot_table = (
        jnp.full((EXPERTS * CAP,), pair_count, jnp.int32)
        .at[target]
        .set(jnp.arange(pair_count, dtype=jnp.int32))
    )
    token_of_slot = slot_table // 2
    gate_flat = jnp.concatenate([route_gates.reshape(-1), jnp.zeros((1,), jnp.float32)])
    slot_gate = gate_flat[slot_table][:, None]
    gates_wide = route_gates[:, :, None]
    width = tokens.shape[1]
    x_pad = jnp.concatenate([tokens, jnp.zeros((1, width), jnp.bfloat16)], axis=0)
    dy_pad = jnp.concatenate([cotangent, jnp.zeros((1, width), jnp.bfloat16)], axis=0)
    x_sent = x_pad[token_of_slot].reshape(ep_count, local_experts, CAP, width)
    dy_rows = (slot_gate * dy_pad[token_of_slot].astype(jnp.float32)).astype(jnp.bfloat16)
    x_sent, dy_sent = (x_sent, dy_rows.reshape(ep_count, local_experts, CAP, width))
    x_recv, dy_recv = (
        lax.all_to_all(x_sent, "ep", split_axis=0, concat_axis=2, tiled=True),
        lax.all_to_all(dy_sent, "ep", split_axis=0, concat_axis=2, tiled=True),
    )
    x_rows, dy_rows = (
        lax.all_gather(x_recv, "etp", axis=3, tiled=True),
        lax.all_gather(dy_recv, "etp", axis=3, tiled=True),
    )
    rows_x = x_rows[0]
    rows_dy = dy_rows[0]
    gate_pre = jnp.einsum("erd,edf->erf", rows_x, w_gate, preferred_element_type=jnp.float32)
    up_pre = jnp.einsum("erd,edf->erf", rows_x, w_up, preferred_element_type=jnp.float32)
    sigma = jax.nn.sigmoid(gate_pre)
    hidden = (jax.nn.silu(gate_pre) * up_pre).astype(jnp.bfloat16)
    output_part = jnp.einsum("erf,efd->erd", hidden, w_down, preferred_element_type=jnp.float32)
    d_hidden = jnp.einsum("erd,efd->erf", rows_dy, w_down, preferred_element_type=jnp.float32)
    d_up = (d_hidden * jax.nn.silu(gate_pre)).astype(jnp.bfloat16)
    d_gate = (d_hidden * up_pre * sigma * (1.0 + gate_pre * (1.0 - sigma))).astype(jnp.bfloat16)
    grad_down = jnp.einsum("erf,erd->efd", hidden, rows_dy, preferred_element_type=jnp.float32)
    grad_gate_w = jnp.einsum("erd,erf->edf", rows_x, d_gate, preferred_element_type=jnp.float32)
    grad_up_w = jnp.einsum("erd,erf->edf", rows_x, d_up, preferred_element_type=jnp.float32)
    output_part, grad_w_gate, grad_w_up, grad_w_down = (
        output_part,
        grad_gate_w.astype(jnp.bfloat16),
        grad_up_w.astype(jnp.bfloat16),
        grad_down.astype(jnp.bfloat16),
    )
    returned = lax.all_to_all(output_part[None], "ep", split_axis=2, concat_axis=0, tiled=True)
    pair_rows = returned.reshape(EXPERTS * CAP, -1)[target].reshape(tok_count, 2, -1)
    full_rows = lax.psum_scatter(pair_rows, "etp", scatter_dimension=2, tiled=True)
    mixed = jnp.sum(gates_wide * full_rows, axis=1).astype(jnp.bfloat16)
    partial_grad = jnp.sum(full_rows * cotangent.astype(jnp.float32)[:, None, :], axis=2)
    grad_gates = lax.psum(partial_grad, "etp")
    return (mixed, grad_gates, grad_w_gate, grad_w_up, grad_w_down)


def solution(mesh):
    in_specs = (
        P("ep", "etp"),
        P("ep", None),
        P("ep", None),
        P("ep", "etp"),
        P("ep", None, "etp"),
        P("ep", None, "etp"),
        P("ep", "etp", None),
    )
    out_specs = (
        P("ep", "etp"),
        P("ep", None),
        P("ep", None, "etp"),
        P("ep", None, "etp"),
        P("ep", "etp", None),
    )
    return jax.shard_map(
        per_device, mesh=mesh, in_specs=in_specs, out_specs=out_specs, check_vma=False
    )
```

profile of v0, /device:TPU:8, one launch (start us, length us, event | category | flops | bytes accessed | tf_op | source)
XLA Modules:
  0.0 672.6 jit_solution(16049948253081429663)
XLA Ops:
  7.2 0.8 broadcast_multiply_fusion
  9.6 0.9 scatter_custom_fusion
  11.2 0.8 gather_fusion
  12.1 14.6 %all_to_all.33 = bf16[8,2,576]{2,1,0:T(2,128)(2,1)S(1)} all-to-all(bf16[8,2,576]{2,1,0:T(2,128)(2,1)S(1)} %reshape.210), channel_id=1, replica_groups=mesh['ep'=8,'etp'=64] {'ep'}, dimensions={0} | all-to-all | bytes 36864 | tf_op jit(solution)/shard_map/all_to_all | solution.py:36
  27.5 0.8 copy.20
  29.0 0.8 gather_fusion.3
  30.0 1.6 gather_fusion.2
  32.5 4.6 all-to-all-start.2
  37.1 73.1 %all-gather.3.cloned.1.call-done = bf16[1,1,192,3072]{2,3,1,0:T(8,128)(2,1)} async-done(((bf16[1,1,192,48]{2,3,1,0:T(8,128)(2,1)}), bf16[1,1,192,3072]{2,3,1,0:T(8,128)(2,1)}) %all-gather.3.cloned.1.call-update) | async-done | bytes 1179664 | tf_op jit(solution)/shard_map/all_gather | solution.py:40
  110.2 2.1 fusion.10
  113.5 3.8 copy.25
  117.3 7.4 %all-to-all-start.1 = ((f32[1,1,192,3072]{3,1,0,2:T(1,128)}), f32[1,1,192,3072]{3,1,0,2:T(1,128)}, u32[]{:S(2)}, u32[]{:S(2)}) async-start(f32[1,1,192,3072]{3,1,0,2:T(1,128)} %copy.25), calls=%async_computation.1 | async-start | bytes 4718592 | tf_op jit(solution)/shard_map/all_to_all | solution.py:62
  125.6 1.3 dynamic-slice
  127.6 82.1 %all-gather.5.cloned.1.call-done = bf16[1,1,192,3072]{2,3,1,0:T(8,128)(2,1)} async-done(((bf16[1,1,192,48]{2,3,1,0:T(8,128)(2,1)}), bf16[1,1,192,3072]{2,3,1,0:T(8,128)(2,1)}) %all-gather.5.cloned.1.call-update) | async-done | bytes 1179664 | tf_op jit(solution)/shard_map/all_gather | solution.py:41
  209.7 2.0 fusion.4
  211.7 2.1 copy.34
  213.8 2.0 gather_fusion.1
  215.8 2.9 reshape.158
  218.7 3.1 fusion.2
  221.8 1.5 fusion.1
  223.3 1.5 fusion
  224.7 189.6 %all-reduce.5.cloned.1.call-done = f32[48,2,3072]{2,1,0:T(2,128)} async-done(((f32[48,2,3072]{2,1,0:T(2,128)}), f32[48,2,3072]{2,1,0:T(2,128)}) %all-reduce.5.cloned.1.call-update) | async-done | bytes 1179664
  414.3 1.7 multiply_reduce_fusion
  416.1 249.4 %psum.7 = f32[48,2]{1,0:T(8,128)S(1)} all-reduce(f32[48,2]{1,0:T(8,128)S(1)} %get-tuple-element.10), channel_id=1, replica_groups=mesh['ep'=8,'etp'=64] {'etp'}, use_global_device_ids=true, to_apply=%region_6.7 | all-reduce | flops 96 | bytes 768 | tf_op jit(solution)/shard_map/psum | solution.py:67
  (48 shorter events, 7.7 us)
Async XLA Ops:
  7.2 105.8 %copy-start = (bf16[1,128,3072]{2,1,0:T(8,128)(2,1)S(1)}, bf16[1,128,3072]{2,1,0:T(8,128)(2,1)}, u32[]{:S(2)}) copy-start(bf16[1,128,3072]{2,1,0:T(8,128)(2,1)} %param.13) | copy-start | bytes 2359300
  7.2 103.0 %copy-start.3 = (bf16[1,3072,128]{2,1,0:T(8,128)(2,1)S(1)}, bf16[1,3072,128]{2,1,0:T(8,128)(2,1)}, u32[]{:S(2)}) copy-start(bf16[1,3072,128]{2,1,0:T(8,128)(2,1)} %param.11) | copy-start | bytes 2359300
  7.2 103.0 %all-gather.3.cloned.1.call-start = ((), (), s32[]{:S(2)}) async-start(), calls=%async_computation.3 | async-start | bytes 1597440 | tf_op jit(solution)/shard_map/all_gather | solution.py:40
  31.5 80.8 %copy-start.5 = (bf16[1,3072,128]{2,1,0:T(8,128)(2,1)S(1)}, bf16[1,3072,128]{2,1,0:T(8,128)(2,1)}, u32[]{:S(2)}) copy-start(bf16[1,3072,128]{2,1,0:T(8,128)(2,1)} %param.12) | copy-start | bytes 2359300
  32.5 84.8 %all-to-all-start.2 = ((bf16[8,2,576]{2,1,0:T(2,128)(2,1)}), bf16[8,2,576]{2,1,0:T(2,128)(2,1)S(1)}, u32[]{:S(2)}, u32[]{:S(2)}) async-start(bf16[8,2,576]{2,1,0:T(2,128)(2,1)} %reshape.212), calls=%async_computation.2 | async-start | bytes 40960 | tf_op jit(solution)/shard_map/all_to_all | solution.py:37
  110.2 2.1 copy-start.1
  117.3 8.3 %copy-start.4 = (bf16[48,48]{1,0:T(8,128)(2,1)S(1)}, bf16[48,48]{1,0:T(8,128)(2,1)}, u32[]{:S(2)}) copy-start(bf16[48,48]{1,0:T(8,128)(2,1)} %param.10) | copy-start | bytes 13828
  117.3 94.4 %all-to-all-start.1 = ((f32[1,1,192,3072]{3,1,0,2:T(1,128)}), f32[1,1,192,3072]{3,1,0,2:T(1,128)}, u32[]{:S(2)}, u32[]{:S(2)}) async-start(f32[1,1,192,3072]{3,1,0,2:T(1,128)} %copy.25), calls=%async_computation.1 | async-start | bytes 4718592 | tf_op jit(solution)/shard_map/all_to_all | solution.py:62
  124.7 85.0 %all-gather.5.cloned.1.call-start = ((), (), s32[]{:S(2)}) async-start(), calls=%async_computation.4 | async-start | bytes 1597440 | tf_op jit(solution)/shard_map/all_gather | solution.py:41
  125.5 288.8 %all-reduce.5.cloned.1.call-start = ((), (), s32[]{:S(2)}) async-start(), calls=%async_computation.5 | async-start | bytes 2359296
  218.7 3.1 copy-start.2
Sparse Core Ops, SparseCore 0:
  27.6 82.5 all-gather.2
  129.4 80.2 all-gather.4
  218.9 195.4 all-reduce.4
where the time goes:
time: 673 us
  waiting for transfers between devices  345 us (51%)
  blocking collectives  264 us (39%)
  local copies, waits for them, and re-layouts  22.7 us (3%)
  between operations  14.6 us (2%)
  starting transfers between devices  12.1 us (2%)
  matrix products  11.2 us (2%)
    psum x1, blocking collectives, per_device(): grad_gates = lax.psum(partial_grad, 'etp')  249 us
    unnamed x4, waiting for transfers between devices  190 us
    all_gather x1, waiting for transfers between devices, per_device(): lax.all_gather(dy_recv, 'etp', axis=3, tiled=True)  82.1 us
    all_gather x1, waiting for transfers between devices, per_device(): lax.all_gather(x_recv, 'etp', axis=3, tiled=True)  73.1 us
    all_to_all x1, blocking collectives, per_device(): lax.all_to_all(x_sent, 'ep', split_axis=0, concat_axis=2, tiled=True)  14.6 us
  transfers between devices with their start and end apart: 5, of which 3 were waited for; matrix products, arithmetic and copies ran while one was open for 3% of the time, Pallas kernels for 0%

commit v1 on v0

--- a/solution.py
+++ b/solution.py
@@ -5,6 +5,11 @@
 
 EXPERTS = 8
 CAP = 24
+
+
+def all_by_exchange(block, axis, along):
+    sent = jnp.stack([block] * lax.axis_size(axis))
+    return jnp.concatenate(lax.all_to_all(sent, axis, 0, 0), axis=along)
 
 
 def per_device(tokens, routes, route_gates, cotangent, w_gate, w_up, w_down):
@@ -38,7 +43,7 @@
     )
     x_rows, dy_rows = (
         lax.all_gather(x_recv, "etp", axis=3, tiled=True),
-        lax.all_gather(dy_recv, "etp", axis=3, tiled=True),
+        all_by_exchange(dy_recv, "etp", 3),
     )
     rows_x = x_rows[0]
     rows_dy = dy_rows[0]

time: 673 us -> 641 us (0.952)
  waiting for transfers between devices: 345 us -> 295 us
  blocking collectives: 264 us -> 274 us
  starting transfers between devices: 12.1 us -> 19.9 us
    all_gather x1 -> x0, waiting for transfers between devices: 82.1 us -> none  [per_device(): lax.all_gather(dy_recv, 'etp', axis=3, tiled=True)]
    all_to_all x1, waiting for transfers between devices: 0.01 us -> 53.3 us  [per_device(): lax.all_to_all(output_part[None], 'ep', split_axis=2, concat_axis=0, tile...]
    all_gather x1, waiting for transfers between devices: 73.1 us -> 55.5 us  [per_device(): lax.all_gather(x_recv, 'etp', axis=3, tiled=True)]
    all_to_all x0 -> x1, blocking collectives: none -> 10.2 us  [per_device(): lax.all_to_all(dy_sent, 'ep', split_axis=0, concat_axis=2, tiled=True)]
    all_to_all x1, starting transfers between devices: 4.64 us -> 13.1 us  [all_by_exchange(): return jnp.concatenate(lax.all_to_all(sent, axis, 0, 0), axis=along)]
    unnamed x4 -> x3, waiting for transfers between devices: 190 us -> 187 us
  transfers between devices with their start and end apart: 5 -> 4, of which waited for: 3 -> 3; matrix products, arithmetic and copies ran while one was open for 3% -> 3% of each run, Pallas kernels for 0% -> 0%
where the time goes in v1:
time: 641 us; the launch traced here: 640 us
  waiting for transfers between devices  295 us (46%)
  blocking collectives  274 us (43%)
  local copies, waits for them, and re-layouts  22.8 us (4%)
  starting transfers between devices  19.9 us (3%)
  between operations  14.9 us (2%)
  matrix products  9.8 us (2%)
    psum x1, blocking collectives, per_device(): grad_gates = lax.psum(partial_grad, 'etp')  249 us
    unnamed x3, waiting for transfers between devices  187 us
    all_gather x1, waiting for transfers between devices, per_device(): lax.all_gather(x_recv, 'etp', axis=3, tiled=True)  55.5 us
    all_to_all x1, waiting for transfers between devices, per_device(): lax.all_to_all(output_part[None], 'ep', split_axis=2, concat_axis=0, tile...  53.3 us
    all_to_all x1, blocking collectives, per_device(): lax.all_to_all(x_sent, 'ep', split_axis=0, concat_axis=2, tiled=True)  14.6 us
    all_to_all x1, starting transfers between devices, all_by_exchange(): return jnp.concatenate(lax.all_to_all(sent, axis, 0, 0), axis=along)  13.1 us
  transfers between devices with their start and end apart: 4, of which 3 were waited for; matrix products, arithmetic and copies ran while one was open for 3% of the time, Pallas kernels for 0%

profile of v1, /device:TPU:8, one launch (start us, length us, event | category | flops | bytes accessed | tf_op | source)
XLA Modules:
  0.0 639.9 jit_solution(4001386453044065437)
XLA Ops:
  9.5 0.9 scatter_custom_fusion
  11.1 0.8 gather_fusion
  12.0 14.6 %all_to_all.35 = bf16[8,2,576]{2,1,0:T(2,128)(2,1)S(1)} all-to-all(bf16[8,2,576]{2,1,0:T(2,128)(2,1)S(1)} %reshape.219), channel_id=1, replica_groups=mesh['ep'=8,'etp'=64] {'ep'}, dimensions={0} | all-to-all | bytes 36864 | tf_op jit(solution)/shard_map/all_to_all | solution.py:41
  27.5 0.8 copy.21
  28.9 0.8 gather_fusion.3
  29.9 1.6 gather_fusion.2
  31.8 10.2 %all_to_all.36 = bf16[8,2,576]{2,1,0:T(2,128)(2,1)S(1)} all-to-all(bf16[8,2,576]{2,1,0:T(2,128)(2,1)S(1)} %reshape.221), channel_id=1, replica_groups=mesh['ep'=8,'etp'=64] {'ep'}, dimensions={0} | all-to-all | bytes 36864 | tf_op jit(solution)/shard_map/all_to_all | solution.py:42
  42.2 1.3 stack.5
  43.4 13.1 %all-to-all-start.3 = ((bf16[64,1,1,192,48]{3,4,2,1,0:T(8,128)(2,1)}), bf16[64,1,1,192,48]{3,4,2,1,0:T(8,128)(2,1)S(1)}, u32[]{:S(2)}, u32[]{:S(2)}) async-start(bf16[64,1,1,192,48]{3,4,2,1,0:T(8,128)(2,1)} %stack.5), calls=%async_computation.3 | async-start | bytes 3145728 | tf_op jit(solution)/shard_map/all_to_all | solution.py:12
  56.5 55.5 %all-gather.2.cloned.1.call-done = bf16[1,1,192,3072]{2,3,1,0:T(8,128)(2,1)} async-done(((bf16[1,1,192,48]{2,3,1,0:T(8,128)(2,1)}), bf16[1,1,192,3072]{2,3,1,0:T(8,128)(2,1)}) %all-gather.2.cloned.1.call-update) | async-done | bytes 1179664 | tf_op jit(solution)/shard_map/all_gather | solution.py:45
  112.0 2.2 fusion.7
  115.3 3.8 copy.26
  119.1 6.8 %all-to-all-start.1 = ((f32[1,1,192,3072]{3,1,0,2:T(1,128)}), f32[1,1,192,3072]{3,1,0,2:T(1,128)}, u32[]{:S(2)}, u32[]{:S(2)}) async-start(f32[1,1,192,3072]{3,1,0,2:T(1,128)} %copy.26), calls=%async_computation.1 | async-start | bytes 4718592 | tf_op jit(solution)/shard_map/all_to_all | solution.py:67
  125.9 1.3 dynamic-slice
  128.5 53.3 %all-to-all-done.1 = f32[1,1,192,3072]{3,1,0,2:T(1,128)} async-done(((f32[1,1,192,3072]{3,1,0,2:T(1,128)}), f32[1,1,192,3072]{3,1,0,2:T(1,128)}, u32[]{:S(2)}, u32[]{:S(2)}) %all-to-all-start.1) | async-done | bytes 2359328 | tf_op jit(solution)/shard_map/all_to_all | solution.py:67
  181.8 2.1 copy.35
  183.9 2.0 gather_fusion.1
  185.9 2.9 reshape.166
  188.8 3.1 fusion.2
  191.9 1.5 fusion.1
  193.4 1.5 fusion
  194.8 186.5 %all-reduce.5.cloned.1.call-done = f32[48,2,3072]{2,1,0:T(2,128)} async-done(((f32[48,2,3072]{2,1,0:T(2,128)}), f32[48,2,3072]{2,1,0:T(2,128)}) %all-reduce.5.cloned.1.call-update) | async-done | bytes 1179664
  381.3 1.7 multiply_reduce_fusion
  383.1 249.4 %psum.7 = f32[48,2]{1,0:T(8,128)S(1)} all-reduce(f32[48,2]{1,0:T(8,128)S(1)} %get-tuple-element.10), channel_id=1, replica_groups=mesh['ep'=8,'etp'=64] {'etp'}, use_global_device_ids=true, to_apply=%region_6.7 | all-reduce | flops 96 | bytes 768 | tf_op jit(solution)/shard_map/psum | solution.py:72
  (49 shorter events, 7.7 us)
Async XLA Ops:
  7.2 107.6 %copy-start = (bf16[1,128,3072]{2,1,0:T(8,128)(2,1)S(1)}, bf16[1,128,3072]{2,1,0:T(8,128)(2,1)}, u32[]{:S(2)}) copy-start(bf16[1,128,3072]{2,1,0:T(8,128)(2,1)} %param.13) | copy-start | bytes 2359300
  7.2 104.8 %all-gather.2.cloned.1.call-start = ((), (), s32[]{:S(2)}) async-start(), calls=%async_computation.4 | async-start | bytes 1597440 | tf_op jit(solution)/shard_map/all_gather | solution.py:45
  43.4 68.6 %copy-start.4 = (bf16[1,3072,128]{2,1,0:T(8,128)(2,1)S(1)}, bf16[1,3072,128]{2,1,0:T(8,128)(2,1)}, u32[]{:S(2)}) copy-start(bf16[1,3072,128]{2,1,0:T(8,128)(2,1)} %param.11) | copy-start | bytes 2359300
  43.4 75.7 %all-to-all-start.3 = ((bf16[64,1,1,192,48]{3,4,2,1,0:T(8,128)(2,1)}), bf16[64,1,1,192,48]{3,4,2,1,0:T(8,128)(2,1)S(1)}, u32[]{:S(2)}, u32[]{:S(2)}) async-start(bf16[64,1,1,192,48]{3,4,2,1,0:T(8,128)(2,1)} %stack.5), calls=%async_computation.3 | async-start | bytes 3145728 | tf_op jit(solution)/shard_map/all_to_all | solution.py:12
  112.0 2.2 copy-start.1
  112.0 2.2 copy-start.6
  119.1 6.8 %copy-start.5 = (bf16[48,48]{1,0:T(8,128)(2,1)S(1)}, bf16[48,48]{1,0:T(8,128)(2,1)}, u32[]{:S(2)}) copy-start(bf16[48,48]{1,0:T(8,128)(2,1)} %param.10) | copy-start | bytes 13828
  119.1 8.7 %copy-start.3 = (bf16[64,1,1,192,48]{3,4,2,1,0:T(8,128)(2,1)}, bf16[64,1,1,192,48]{3,4,2,1,0:T(8,128)(2,1)S(1)}, u32[]{:S(2)}) copy-start(bf16[64,1,1,192,48]{3,4,2,1,0:T(8,128)(2,1)S(1)} %all-to-all-done.3) | copy-start | bytes 3538948
  119.1 62.7 %all-to-all-start.1 = ((f32[1,1,192,3072]{3,1,0,2:T(1,128)}), f32[1,1,192,3072]{3,1,0,2:T(1,128)}, u32[]{:S(2)}, u32[]{:S(2)}) async-start(f32[1,1,192,3072]{3,1,0,2:T(1,128)} %copy.26), calls=%async_computation.1 | async-start | bytes 4718592 | tf_op jit(solution)/shard_map/all_to_all | solution.py:67
  125.9 255.4 %all-reduce.5.cloned.1.call-start = ((), (), s32[]{:S(2)}) async-start(), calls=%async_computation.5 | async-start | bytes 2359296
  188.8 3.1 copy-start.2
Sparse Core Ops, SparseCore 0:
  27.6 84.3 all-gather.1
  189.0 192.3 all-reduce.4
